TPU v7x, 32 devices: a whole 2x2x4 slice. The times are simulated.
32 devices in a mesh: group: 2 (over y), tm: 8 (over z, core), pix: 2 (over x), sub: 1.
Axes of the slice: x: 2, y: 2, z: 4, core: 2. Of those that a mesh axis runs over, the one named last changes fastest.
Arguments:
- anomaly: bfloat16 [512, 65536], P('tm', ('group', 'pix', 'sub')), parts along dimension 1, may hold values from -6 to 6
- offsets: int32 [32], replicated, may hold values from 0 to 256, as said below
- taper_index: int32 [32], replicated, may hold values from 0 to 3
Outputs:
- spectral_gram: float32 [256, 64, 64], P(('group', 'tm')), parts along dimension 0
- leading_energy: float32 [256], P(('group', 'tm')), parts along dimension 0
There are 2 independent parts, one for each index of `group`. A program takes and returns all parts, laid end to end along the dimension named above; an argument that names none is the same for every part. Nothing has to cross between parts.
Inputs may be any that keep to these rules, and one draw needn't show every extreme that they name: `offsets`: block starts never fall; the first block starts at day 0 and the last at day 512 - 256.
All inputs are finite; a program needn't handle non-finite values.
Results may differ from a plain program's by a relative error of at most 0.0034.
Values may be sent and summed in bfloat16 or wider, within the bound.
A program may use at most 128 MiB of HBM per device.

v0:
```python
import math
import jax
import jax.numpy as jnp
from jax import lax
from jax.sharding import PartitionSpec as P

NFFT = 256
NB = 32
POWER = 8
NF = 128
power_eps = 1e-06


def window_rows(taper_index, length):
    steps_t = jnp.arange(length, dtype=jnp.float32)
    phase = steps_t * (2.0 * math.pi / length)
    center = (steps_t + 0.5) * (math.pi / length)
    hann = jnp.sin(center) ** 2
    hamming = 0.54 - 0.46 * jnp.cos(phase)
    blackman = 0.42 - 0.5 * jnp.cos(phase) + 0.08 * jnp.cos(2.0 * phase)
    sine_win = jnp.sin(center)
    table_rows = jnp.stack([hann, hamming, blackman, sine_win])
    chosen = jnp.zeros((taper_index.shape[0], length), jnp.float32)
    for which in range(4):
        chosen = chosen + jnp.where(
            taper_index[:, None] == which, table_rows[which][None, :], jnp.float32(0.0)
        )
    return chosen


def dft_table(length, kept):
    freqs = jnp.arange(kept, dtype=jnp.int32)
    times = jnp.arange(length, dtype=jnp.int32)
    product = freqs[:, None] * times[None, :] % length
    angle = product.astype(jnp.float32) * (2.0 * math.pi / length)
    return jnp.stack([jnp.cos(angle), -jnp.sin(angle)]).astype(jnp.bfloat16)


def local_gram(spectra):
    stacked = spectra.reshape(2 * spectra.shape[1], spectra.shape[2], spectra.shape[3])
    return jnp.einsum("ifp,jfp->fij", stacked, stacked, preferred_element_type=jnp.float32)


def shards(anomaly, offsets, taper_index):
    series = lax.all_to_all(anomaly, "tm", split_axis=1, concat_axis=0, tiled=True)
    windows = window_rows(taper_index, NFFT)
    energy = 1.0 / jnp.sqrt(jnp.sum(windows * windows, axis=1))
    transform = dft_table(NFFT, NF)
    width_here = series.shape[1]
    per_group = 8
    gram_width = 2 * NB

    def fill_group(position, buffer):
        first_block = position * per_group
        starts = lax.dynamic_slice_in_dim(offsets, first_block, per_group, 0)
        shapes = lax.dynamic_slice_in_dim(windows, first_block, per_group, 0)
        scales = lax.dynamic_slice_in_dim(energy, first_block, per_group, 0)
        segments = jax.vmap(lambda first_day: lax.dynamic_slice_in_dim(series, first_day, NFFT, 0))(
            starts
        )
        windowed = (segments * shapes[:, :, None]).astype(jnp.bfloat16)
        spectra = jnp.einsum(
            "rkt,btp->rbkp", transform, windowed, preferred_element_type=jnp.float32
        )
        spectra = (spectra * scales[None, :, None, None]).astype(jnp.bfloat16)
        return lax.dynamic_update_slice_in_dim(buffer, spectra, first_block, 1)

    empty = jnp.zeros((2, NB, NF, width_here), jnp.bfloat16)
    spectra = lax.fori_loop(0, NB // per_group, fill_group, empty)
    received = lax.all_to_all(spectra, "tm", split_axis=2, concat_axis=3, tiled=True)
    partial_value = local_gram(received)
    summed = lax.psum(partial_value, ("pix", "sub"))
    total_pixels = anomaly.shape[1] * lax.axis_size(("pix", "sub"))
    spectral_gram = summed / total_pixels
    vector = jnp.ones((spectral_gram.shape[0], gram_width), jnp.float32)
    for _ in range(POWER):
        applied = jnp.einsum("fij,fj->fi", spectral_gram, vector, precision=lax.Precision.HIGHEST)
        vector = applied / jnp.sqrt(jnp.mean(applied * applied, axis=1, keepdims=True) + power_eps)
    applied = jnp.einsum("fij,fj->fi", spectral_gram, vector, precision=lax.Precision.HIGHEST)
    leading_energy = jnp.sqrt(jnp.mean(applied * applied, axis=1))
    return (spectral_gram, leading_energy)


def solution(mesh):
    placed = (P("tm", ("group", "pix", "sub")), P(), P())
    return jax.shard_map(
        shards,
        mesh=mesh,
        in_specs=placed,
        out_specs=(P(("group", "tm"), None, None), P(("group", "tm"))),
        check_vma=False,
    )
```

profile of v0, /device:TPU:0, one launch (start us, length us, event | category | flops | bytes accessed | tf_op | source)
XLA Modules:
  0.0 1170.2 jit_solution(9330474396484308255)
XLA Ops:
  7.2 3.2 copy.48
  10.4 6.3 all-to-all-start
  18.3 47.5 %all-to-all-done = bf16[64,8,2048]{2,0,1:T(8,128)(2,1)S(1)} async-done(((bf16[64,8,2048]{2,0,1:T(8,128)(2,1)}), bf16[64,8,2048]{2,0,1:T(8,128)(2,1)S(1)}, u32[]{:S(2)}, u32[]{:S(2)}) %all-to-all-start) | async-done | bytes 2097184 | tf_op jit(solution)/shard_map/all_to_all | solution.py:45
  65.8 11.0 broadcast_in_dim.86.clone
  76.7 208.3 %while.16 = (s32[]{:T(128)}, bf16[2,32,128,2048]{3,1,0,2:T(8,128)(2,1)}, s32[32]{0:T(128)S(1)}, bf16[512,2048]{1,0:T(8,128)(2,1)S(1)}, f32[32,256]{1,0:T(8,128)S...) while((s32[]{:T(128)}, ...), condition=%wide.region_2.3_spmd, body=%wide.region_1.2_spmd.sunk | while | flops 2168455168 | bytes 52586048 | solution.py:69
  76.8 19.1 %while.17 = (s32[]{:T(128)}, bf16[512,2048]{1,0:T(8,128)(2,1)S(1)}, s32[8,2]{0,1:T(2,128)S(1)}, bf16[8,256,2048]{2,1,0:T(8,128)(2,1)}, s32[]{:T(128)}) while((s32[]{:T(128)}, bf16[512,2048]{1,0:T(8,128)(2,1)S(1)}, s32[8,2]{0,1:T(2,128)S(1)}, bf16[8,256,2048]{2,1,0:T(8,128)(2,1)}, s32[]{:T(128)}) %tuple.54), condition=%wide.while_cond, body=%wide.while_body.sunk | while | flops 2 | bytes 2098265 | solution.py:58
  79.7 1.9 bitcast_dynamic-update-slice_fusion.2
  89.3 1.8 bitcast_dynamic-update-slice_fusion.2
  96.0 12.1 %fusion.53 = bf16[2,8,128,2048]{2,3,0,1:T(8,128)(2,1)} fusion(f32[8]{0:T(128)S(1)} %dynamic_slice.28, bf16[8,256,2048]{2,1,0:T(8,128)(2,1)} %get-tuple-element.242, f32[8,256]{1,0:T(8,128)S(1)} %constant_dynamic-slice_fusion.4, bf16[2,128,256]{2,1,0:T(8,128)(2,1)S(1)} %get-tuple-element.292), kind=kOutput, calls=%fused_computation.6.clone.1 | convolution fusion | flops 2168455168 | bytes 16916512 | tf_op jit(solution)/shard_map/while/body/eval_jaxpr/rkt,btp->rbkp/dot_general | solution.py:62
  108.0 12.6 %copy.50 = bf16[2,8,128,2048]{3,1,0,2:T(8,128)(2,1)} copy(bf16[2,8,128,2048]{2,3,0,1:T(8,128)(2,1)} %fusion.53) | data formatting | bytes 16777216 | tf_op jit(solution)/shard_map/while/body/eval_jaxpr/dynamic_update_slice | solution.py:66
  120.6 8.2 constant_dynamic-update-slice_fusion.2
  128.9 19.1 %while.17 = (s32[]{:T(128)}, bf16[512,2048]{1,0:T(8,128)(2,1)S(1)}, s32[8,2]{0,1:T(2,128)S(1)}, bf16[8,256,2048]{2,1,0:T(8,128)(2,1)}, s32[]{:T(128)}) while((s32[]{:T(128)}, bf16[512,2048]{1,0:T(8,128)(2,1)S(1)}, s32[8,2]{0,1:T(2,128)S(1)}, bf16[8,256,2048]{2,1,0:T(8,128)(2,1)}, s32[]{:T(128)}) %tuple.54), condition=%wide.while_cond, body=%wide.while_body.sunk | while | flops 2 | bytes 2098265 | solution.py:58
  131.8 1.9 bitcast_dynamic-update-slice_fusion.2
  141.3 1.8 bitcast_dynamic-update-slice_fusion.2
  148.0 12.1 %fusion.53 = bf16[2,8,128,2048]{2,3,0,1:T(8,128)(2,1)} fusion(f32[8]{0:T(128)S(1)} %dynamic_slice.28, bf16[8,256,2048]{2,1,0:T(8,128)(2,1)} %get-tuple-element.242, f32[8,256]{1,0:T(8,128)S(1)} %constant_dynamic-slice_fusion.4, bf16[2,128,256]{2,1,0:T(8,128)(2,1)S(1)} %get-tuple-element.292), kind=kOutput, calls=%fused_computation.6.clone.1 | convolution fusion | flops 2168455168 | bytes 16916512 | tf_op jit(solution)/shard_map/while/body/eval_jaxpr/rkt,btp->rbkp/dot_general | solution.py:62
  160.1 12.6 %copy.50 = bf16[2,8,128,2048]{3,1,0,2:T(8,128)(2,1)} copy(bf16[2,8,128,2048]{2,3,0,1:T(8,128)(2,1)} %fusion.53) | data formatting | bytes 16777216 | tf_op jit(solution)/shard_map/while/body/eval_jaxpr/dynamic_update_slice | solution.py:66
  172.6 8.2 constant_dynamic-update-slice_fusion.2
  181.0 19.1 %while.17 = (s32[]{:T(128)}, bf16[512,2048]{1,0:T(8,128)(2,1)S(1)}, s32[8,2]{0,1:T(2,128)S(1)}, bf16[8,256,2048]{2,1,0:T(8,128)(2,1)}, s32[]{:T(128)}) while((s32[]{:T(128)}, bf16[512,2048]{1,0:T(8,128)(2,1)S(1)}, s32[8,2]{0,1:T(2,128)S(1)}, bf16[8,256,2048]{2,1,0:T(8,128)(2,1)}, s32[]{:T(128)}) %tuple.54), condition=%wide.while_cond, body=%wide.while_body.sunk | while | flops 2 | bytes 2098265 | solution.py:58
  183.9 1.9 bitcast_dynamic-update-slice_fusion.2
  200.1 12.1 %fusion.53 = bf16[2,8,128,2048]{2,3,0,1:T(8,128)(2,1)} fusion(f32[8]{0:T(128)S(1)} %dynamic_slice.28, bf16[8,256,2048]{2,1,0:T(8,128)(2,1)} %get-tuple-element.242, f32[8,256]{1,0:T(8,128)S(1)} %constant_dynamic-slice_fusion.4, bf16[2,128,256]{2,1,0:T(8,128)(2,1)S(1)} %get-tuple-element.292), kind=kOutput, calls=%fused_computation.6.clone.1 | convolution fusion | flops 2168455168 | bytes 16916512 | tf_op jit(solution)/shard_map/while/body/eval_jaxpr/rkt,btp->rbkp/dot_general | solution.py:62
  212.2 12.6 %copy.50 = bf16[2,8,128,2048]{3,1,0,2:T(8,128)(2,1)} copy(bf16[2,8,128,2048]{2,3,0,1:T(8,128)(2,1)} %fusion.53) | data formatting | bytes 16777216 | tf_op jit(solution)/shard_map/while/body/eval_jaxpr/dynamic_update_slice | solution.py:66
  224.7 8.2 constant_dynamic-update-slice_fusion.2
  233.0 19.1 %while.17 = (s32[]{:T(128)}, bf16[512,2048]{1,0:T(8,128)(2,1)S(1)}, s32[8,2]{0,1:T(2,128)S(1)}, bf16[8,256,2048]{2,1,0:T(8,128)(2,1)}, s32[]{:T(128)}) while((s32[]{:T(128)}, bf16[512,2048]{1,0:T(8,128)(2,1)S(1)}, s32[8,2]{0,1:T(2,128)S(1)}, bf16[8,256,2048]{2,1,0:T(8,128)(2,1)}, s32[]{:T(128)}) %tuple.54), condition=%wide.while_cond, body=%wide.while_body.sunk | while | flops 2 | bytes 2098265 | solution.py:58
  236.0 1.9 bitcast_dynamic-update-slice_fusion.2
  252.2 12.1 %fusion.53 = bf16[2,8,128,2048]{2,3,0,1:T(8,128)(2,1)} fusion(f32[8]{0:T(128)S(1)} %dynamic_slice.28, bf16[8,256,2048]{2,1,0:T(8,128)(2,1)} %get-tuple-element.242, f32[8,256]{1,0:T(8,128)S(1)} %constant_dynamic-slice_fusion.4, bf16[2,128,256]{2,1,0:T(8,128)(2,1)S(1)} %get-tuple-element.292), kind=kOutput, calls=%fused_computation.6.clone.1 | convolution fusion | flops 2168455168 | bytes 16916512 | tf_op jit(solution)/shard_map/while/body/eval_jaxpr/rkt,btp->rbkp/dot_general | solution.py:62
  264.2 12.6 %copy.50 = bf16[2,8,128,2048]{3,1,0,2:T(8,128)(2,1)} copy(bf16[2,8,128,2048]{2,3,0,1:T(8,128)(2,1)} %fusion.53) | data formatting | bytes 16777216 | tf_op jit(solution)/shard_map/while/body/eval_jaxpr/dynamic_update_slice | solution.py:66
  276.8 8.2 constant_dynamic-update-slice_fusion.2
  285.0 736.0 %all_to_all.34 = bf16[2,32,128,2048]{3,1,0,2:T(8,128)(2,1)} all-to-all(bf16[2,32,128,2048]{3,1,0,2:T(8,128)(2,1)} %get-tuple-element.126), channel_id=1, replica_groups=mesh['group'=2,'tm'=8,'pix'=2,'sub'=1] {'tm'}, dimensions={2} | all-to-all | bytes 67108864 | tf_op jit(solution)/shard_map/all_to_all | solution.py:70
  1021.0 30.0 %copy.21 = bf16[2,32,16,8,2048]{4,3,1,0,2:T(8,128)(2,1)} copy(bf16[2,32,16,8,2048]{4,1,0,2,3:T(8,128)(2,1)} %bitcast.107) | data formatting | bytes 67108864 | tf_op jit(solution)/shard_map/all_to_all | solution.py:70
  1051.0 49.9 %reshape.182 = bf16[64,16,16384]{2,0,1:T(8,128)(2,1)} reshape(bf16[2,32,16,8,2048]{4,3,1,0,2:T(8,128)(2,1)} %copy.21) | data formatting | bytes 67108864 | tf_op jit(solution)/shard_map/reshape | solution.py:40
  1100.9 23.5 %fusion.16 = f32[16,64,64]{2,1,0:T(8,128)} fusion(bf16[64,16,16384]{2,0,1:T(8,128)(2,1)} %reshape.182), kind=kOutput, calls=%fused_computation.64 | convolution fusion | flops 2147483648 | bytes 33816576 | tf_op jit(solution)/shard_map/ifp,jfp->fij/dot_general | solution.py:41
  1124.4 27.1 %all-reduce.3.cloned.1.call-done = f32[16,64,64]{2,1,0:T(8,128)} async-done(((f32[16,64,64]{2,1,0:T(8,128)}), f32[16,64,64]{2,1,0:T(8,128)}) %all-reduce.3.cloned.1.call-update) | async-done | bytes 262160 | tf_op jit(solution)/shard_map/psum | solution.py:72
  (160 shorter events, 79.1 us)
Async XLA Ops:
  10.4 55.4 %all-to-all-start = ((bf16[64,8,2048]{2,0,1:T(8,128)(2,1)}), bf16[64,8,2048]{2,0,1:T(8,128)(2,1)S(1)}, u32[]{:S(2)}, u32[]{:S(2)}) async-start(bf16[64,8,2048]{2,0,1:T(8,128)(2,1)} %bitcast.108), calls=%async_computation | async-start | bytes 4194304 | tf_op jit(solution)/shard_map/all_to_all | solution.py:45
  16.7 1134.8 %all-reduce.3.cloned.1.call-start = ((), (), s32[]{:S(2)}) async-start(), calls=%async_computation.2 | async-start | bytes 1048576 | tf_op jit(solution)/shard_map/psum | solution.py:72
  65.7 11.0 copy-start.1
  1152.6 10.8 copy-start
Sparse Core Ops, SparseCore 0:
  1124.5 26.9 all-reduce.2
where the time goes:
time: 1170 us
  blocking collectives  736 us (63%)
  local copies, waits for them, and re-layouts  254 us (22%)
  matrix products  80.2 us (7%)
  waiting for transfers between devices  74.6 us (6%)
  between operations  14.2 us (1%)
    all_to_all x1, blocking collectives, shards(): lax.all_to_all(spectra, 'tm', split_axis=2, concat_axis=3, tiled=True)  736 us
    dynamic_update_slice x8, local copies, waits for them, and re-layouts, fill_group(): return lax.dynamic_update_slice_in_dim(buffer, spectra, first_block, 1)  83.1 us
    gather x96, local copies, waits for them, and re-layouts  76.2 us
    reshape x1, local copies, waits for them, and re-layouts, local_gram(): spectra.reshape(2 * spectra.shape[1], spectra.shape[2], spectra.shape[3])  49.9 us
    dot_general x4, matrix products, fill_group(): jnp.einsum('rkt,btp->rbkp', transform, windowed, preferred_element_type=j...  48.2 us
    all_to_all x1, waiting for transfers between devices, shards(): lax.all_to_all(anomaly, 'tm', split_axis=1, concat_axis=0, tiled=True)  47.5 us
    all_to_all x1, local copies, waits for them, and re-layouts, shards(): lax.all_to_all(spectra, 'tm', split_axis=2, concat_axis=3, tiled=True)  30 us
    psum x1, waiting for transfers between devices, shards(): summed = lax.psum(partial_value, ('pix', 'sub'))  27.1 us
  transfers between devices with their start and end apart: 2, of which 2 were waited for; matrix products, arithmetic and copies ran while one was open for 0% of the time, Pallas kernels for 0%

commit v1 on v0

--- a/solution.py
+++ b/solution.py
@@ -69,7 +69,8 @@
     spectra = lax.fori_loop(0, NB // per_group, fill_group, empty)
     received = lax.all_to_all(spectra, "tm", split_axis=2, concat_axis=3, tiled=True)
     partial_value = local_gram(received)
-    summed = lax.psum(partial_value, ("pix", "sub"))
+    begin_cycles = lambda panel: lax.psum(lax.psum(panel, axis_name="pix"), "sub")
+    summed = begin_cycles(partial_value)
     total_pixels = anomaly.shape[1] * lax.axis_size(("pix", "sub"))
     spectral_gram = summed / total_pixels
     vector = jnp.ones((spectral_gram.shape[0], gram_width), jnp.float32)

time: 1170 us -> 1170 us (level)
  no operation moved by 1% of the time
where the time goes in v1:
time: 1170 us
  blocking collectives  736 us (63%)
  local copies, waits for them, and re-layouts  254 us (22%)
  matrix products  80.2 us (7%)
  waiting for transfers between devices  74.6 us (6%)
  between operations  14.2 us (1%)
    all_to_all x1, blocking collectives, shards(): lax.all_to_all(spectra, 'tm', split_axis=2, concat_axis=3, tiled=True)  736 us
    dynamic_update_slice x8, local copies, waits for them, and re-layouts, fill_group(): return lax.dynamic_update_slice_in_dim(buffer, spectra, first_block, 1)  83.1 us
    gather x96, local copies, waits for them, and re-layouts  76.2 us
    reshape x1, local copies, waits for them, and re-layouts, local_gram(): spectra.reshape(2 * spectra.shape[1], spectra.shape[2], spectra.shape[3])  49.9 us
    dot_general x4, matrix products, fill_group(): jnp.einsum('rkt,btp->rbkp', transform, windowed, preferred_element_type=j...  48.2 us
    all_to_all x1, waiting for transfers between devices, shards(): lax.all_to_all(anomaly, 'tm', split_axis=1, concat_axis=0, tiled=True)  47.5 us
    all_to_all x1, local copies, waits for them, and re-layouts, shards(): lax.all_to_all(spectra, 'tm', split_axis=2, concat_axis=3, tiled=True)  30 us
    psum x1, waiting for transfers between devices, shards(): lax.psum(panel, axis_name='pix')  27.1 us
  transfers between devices with their start and end apart: 2, of which 2 were waited for; matrix products, arithmetic and copies ran while one was open for 0% of the time, Pallas kernels for 0%

profile of v1, /device:TPU:0, one launch (start us, length us, event | category | flops | bytes accessed | tf_op | source)
XLA Modules:
  0.0 1170.2 jit_solution(9330474396484308255)
XLA Ops:
  7.2 3.2 copy.48
  10.4 6.3 all-to-all-start
  18.3 47.5 %all-to-all-done = bf16[64,8,2048]{2,0,1:T(8,128)(2,1)S(1)} async-done(((bf16[64,8,2048]{2,0,1:T(8,128)(2,1)}), bf16[64,8,2048]{2,0,1:T(8,128)(2,1)S(1)}, u32[]{:S(2)}, u32[]{:S(2)}) %all-to-all-start) | async-done | bytes 2097184 | tf_op jit(solution)/shard_map/all_to_all | solution.py:45
  65.8 11.0 broadcast_in_dim.86.clone
  76.7 208.3 %while.16 = (s32[]{:T(128)}, bf16[2,32,128,2048]{3,1,0,2:T(8,128)(2,1)}, s32[32]{0:T(128)S(1)}, bf16[512,2048]{1,0:T(8,128)(2,1)S(1)}, f32[32,256]{1,0:T(8,128)S...) while((s32[]{:T(128)}, ...), condition=%wide.region_2.3_spmd, body=%wide.region_1.2_spmd.sunk | while | flops 2168455168 | bytes 52586048 | solution.py:69
  76.8 19.1 %while.17 = (s32[]{:T(128)}, bf16[512,2048]{1,0:T(8,128)(2,1)S(1)}, s32[8,2]{0,1:T(2,128)S(1)}, bf16[8,256,2048]{2,1,0:T(8,128)(2,1)}, s32[]{:T(128)}) while((s32[]{:T(128)}, bf16[512,2048]{1,0:T(8,128)(2,1)S(1)}, s32[8,2]{0,1:T(2,128)S(1)}, bf16[8,256,2048]{2,1,0:T(8,128)(2,1)}, s32[]{:T(128)}) %tuple.54), condition=%wide.while_cond, body=%wide.while_body.sunk | while | flops 2 | bytes 2098265 | solution.py:58
  79.7 1.9 bitcast_dynamic-update-slice_fusion.2
  89.3 1.8 bitcast_dynamic-update-slice_fusion.2
  96.0 12.1 %fusion.53 = bf16[2,8,128,2048]{2,3,0,1:T(8,128)(2,1)} fusion(f32[8]{0:T(128)S(1)} %dynamic_slice.28, bf16[8,256,2048]{2,1,0:T(8,128)(2,1)} %get-tuple-element.242, f32[8,256]{1,0:T(8,128)S(1)} %constant_dynamic-slice_fusion.4, bf16[2,128,256]{2,1,0:T(8,128)(2,1)S(1)} %get-tuple-element.292), kind=kOutput, calls=%fused_computation.6.clone.1 | convolution fusion | flops 2168455168 | bytes 16916512 | tf_op jit(solution)/shard_map/while/body/eval_jaxpr/rkt,btp->rbkp/dot_general | solution.py:62
  108.0 12.6 %copy.50 = bf16[2,8,128,2048]{3,1,0,2:T(8,128)(2,1)} copy(bf16[2,8,128,2048]{2,3,0,1:T(8,128)(2,1)} %fusion.53) | data formatting | bytes 16777216 | tf_op jit(solution)/shard_map/while/body/eval_jaxpr/dynamic_update_slice | solution.py:66
  120.6 8.2 constant_dynamic-update-slice_fusion.2
  128.9 19.1 %while.17 = (s32[]{:T(128)}, bf16[512,2048]{1,0:T(8,128)(2,1)S(1)}, s32[8,2]{0,1:T(2,128)S(1)}, bf16[8,256,2048]{2,1,0:T(8,128)(2,1)}, s32[]{:T(128)}) while((s32[]{:T(128)}, bf16[512,2048]{1,0:T(8,128)(2,1)S(1)}, s32[8,2]{0,1:T(2,128)S(1)}, bf16[8,256,2048]{2,1,0:T(8,128)(2,1)}, s32[]{:T(128)}) %tuple.54), condition=%wide.while_cond, body=%wide.while_body.sunk | while | flops 2 | bytes 2098265 | solution.py:58
  131.8 1.9 bitcast_dynamic-update-slice_fusion.2
  141.3 1.8 bitcast_dynamic-update-slice_fusion.2
  148.0 12.1 %fusion.53 = bf16[2,8,128,2048]{2,3,0,1:T(8,128)(2,1)} fusion(f32[8]{0:T(128)S(1)} %dynamic_slice.28, bf16[8,256,2048]{2,1,0:T(8,128)(2,1)} %get-tuple-element.242, f32[8,256]{1,0:T(8,128)S(1)} %constant_dynamic-slice_fusion.4, bf16[2,128,256]{2,1,0:T(8,128)(2,1)S(1)} %get-tuple-element.292), kind=kOutput, calls=%fused_computation.6.clone.1 | convolution fusion | flops 2168455168 | bytes 16916512 | tf_op jit(solution)/shard_map/while/body/eval_jaxpr/rkt,btp->rbkp/dot_general | solution.py:62
  160.1 12.6 %copy.50 = bf16[2,8,128,2048]{3,1,0,2:T(8,128)(2,1)} copy(bf16[2,8,128,2048]{2,3,0,1:T(8,128)(2,1)} %fusion.53) | data formatting | bytes 16777216 | tf_op jit(solution)/shard_map/while/body/eval_jaxpr/dynamic_update_slice | solution.py:66
  172.6 8.2 constant_dynamic-update-slice_fusion.2
  181.0 19.1 %while.17 = (s32[]{:T(128)}, bf16[512,2048]{1,0:T(8,128)(2,1)S(1)}, s32[8,2]{0,1:T(2,128)S(1)}, bf16[8,256,2048]{2,1,0:T(8,128)(2,1)}, s32[]{:T(128)}) while((s32[]{:T(128)}, bf16[512,2048]{1,0:T(8,128)(2,1)S(1)}, s32[8,2]{0,1:T(2,128)S(1)}, bf16[8,256,2048]{2,1,0:T(8,128)(2,1)}, s32[]{:T(128)}) %tuple.54), condition=%wide.while_cond, body=%wide.while_body.sunk | while | flops 2 | bytes 2098265 | solution.py:58
  183.9 1.9 bitcast_dynamic-update-slice_fusion.2
  200.1 12.1 %fusion.53 = bf16[2,8,128,2048]{2,3,0,1:T(8,128)(2,1)} fusion(f32[8]{0:T(128)S(1)} %dynamic_slice.28, bf16[8,256,2048]{2,1,0:T(8,128)(2,1)} %get-tuple-element.242, f32[8,256]{1,0:T(8,128)S(1)} %constant_dynamic-slice_fusion.4, bf16[2,128,256]{2,1,0:T(8,128)(2,1)S(1)} %get-tuple-element.292), kind=kOutput, calls=%fused_computation.6.clone.1 | convolution fusion | flops 2168455168 | bytes 16916512 | tf_op jit(solution)/shard_map/while/body/eval_jaxpr/rkt,btp->rbkp/dot_general | solution.py:62
  212.2 12.6 %copy.50 = bf16[2,8,128,2048]{3,1,0,2:T(8,128)(2,1)} copy(bf16[2,8,128,2048]{2,3,0,1:T(8,128)(2,1)} %fusion.53) | data formatting | bytes 16777216 | tf_op jit(solution)/shard_map/while/body/eval_jaxpr/dynamic_update_slice | solution.py:66
  224.7 8.2 constant_dynamic-update-slice_fusion.2
  233.0 19.1 %while.17 = (s32[]{:T(128)}, bf16[512,2048]{1,0:T(8,128)(2,1)S(1)}, s32[8,2]{0,1:T(2,128)S(1)}, bf16[8,256,2048]{2,1,0:T(8,128)(2,1)}, s32[]{:T(128)}) while((s32[]{:T(128)}, bf16[512,2048]{1,0:T(8,128)(2,1)S(1)}, s32[8,2]{0,1:T(2,128)S(1)}, bf16[8,256,2048]{2,1,0:T(8,128)(2,1)}, s32[]{:T(128)}) %tuple.54), condition=%wide.while_cond, body=%wide.while_body.sunk | while | flops 2 | bytes 2098265 | solution.py:58
  236.0 1.9 bitcast_dynamic-update-slice_fusion.2
  252.2 12.1 %fusion.53 = bf16[2,8,128,2048]{2,3,0,1:T(8,128)(2,1)} fusion(f32[8]{0:T(128)S(1)} %dynamic_slice.28, bf16[8,256,2048]{2,1,0:T(8,128)(2,1)} %get-tuple-element.242, f32[8,256]{1,0:T(8,128)S(1)} %constant_dynamic-slice_fusion.4, bf16[2,128,256]{2,1,0:T(8,128)(2,1)S(1)} %get-tuple-element.292), kind=kOutput, calls=%fused_computation.6.clone.1 | convolution fusion | flops 2168455168 | bytes 16916512 | tf_op jit(solution)/shard_map/while/body/eval_jaxpr/rkt,btp->rbkp/dot_general | solution.py:62
  264.2 12.6 %copy.50 = bf16[2,8,128,2048]{3,1,0,2:T(8,128)(2,1)} copy(bf16[2,8,128,2048]{2,3,0,1:T(8,128)(2,1)} %fusion.53) | data formatting | bytes 16777216 | tf_op jit(solution)/shard_map/while/body/eval_jaxpr/dynamic_update_slice | solution.py:66
  276.8 8.2 constant_dynamic-update-slice_fusion.2
  285.0 736.0 %all_to_all.34 = bf16[2,32,128,2048]{3,1,0,2:T(8,128)(2,1)} all-to-all(bf16[2,32,128,2048]{3,1,0,2:T(8,128)(2,1)} %get-tuple-element.126), channel_id=1, replica_groups=mesh['group'=2,'tm'=8,'pix'=2,'sub'=1] {'tm'}, dimensions={2} | all-to-all | bytes 67108864 | tf_op jit(solution)/shard_map/all_to_all | solution.py:70
  1021.0 30.0 %copy.21 = bf16[2,32,16,8,2048]{4,3,1,0,2:T(8,128)(2,1)} copy(bf16[2,32,16,8,2048]{4,1,0,2,3:T(8,128)(2,1)} %bitcast.107) | data formatting | bytes 67108864 | tf_op jit(solution)/shard_map/all_to_all | solution.py:70
  1051.0 49.9 %reshape.182 = bf16[64,16,16384]{2,0,1:T(8,128)(2,1)} reshape(bf16[2,32,16,8,2048]{4,3,1,0,2:T(8,128)(2,1)} %copy.21) | data formatting | bytes 67108864 | tf_op jit(solution)/shard_map/reshape | solution.py:40
  1100.9 23.5 %fusion.16 = f32[16,64,64]{2,1,0:T(8,128)} fusion(bf16[64,16,16384]{2,0,1:T(8,128)(2,1)} %reshape.182), kind=kOutput, calls=%fused_computation.64 | convolution fusion | flops 2147483648 | bytes 33816576 | tf_op jit(solution)/shard_map/ifp,jfp->fij/dot_general | solution.py:41
  1124.4 27.1 %all-reduce.3.cloned.1.call-done = f32[16,64,64]{2,1,0:T(8,128)} async-done(((f32[16,64,64]{2,1,0:T(8,128)}), f32[16,64,64]{2,1,0:T(8,128)}) %all-reduce.3.cloned.1.call-update) | async-done | bytes 262160 | tf_op jit(solution)/shard_map/psum | solution.py:72
  (160 shorter events, 79.1 us)
Async XLA Ops:
  10.4 55.4 %all-to-all-start = ((bf16[64,8,2048]{2,0,1:T(8,128)(2,1)}), bf16[64,8,2048]{2,0,1:T(8,128)(2,1)S(1)}, u32[]{:S(2)}, u32[]{:S(2)}) async-start(bf16[64,8,2048]{2,0,1:T(8,128)(2,1)} %bitcast.108), calls=%async_computation | async-start | bytes 4194304 | tf_op jit(solution)/shard_map/all_to_all | solution.py:45
  16.7 1134.8 %all-reduce.3.cloned.1.call-start = ((), (), s32[]{:S(2)}) async-start(), calls=%async_computation.2 | async-start | bytes 1048576 | tf_op jit(solution)/shard_map/psum | solution.py:72
  65.7 11.0 copy-start.1
  1152.6 10.8 copy-start
Sparse Core Ops, SparseCore 0:
  1124.5 26.9 all-reduce.2
